TPU v7x, 32 devices: a whole 2x2x4 slice. The times are simulated.
32 devices in a mesh: grp: 4 (over y, x), blk: 8 (over z, core).
Axes of the slice: x: 2, y: 2, z: 4, core: 2. Of those that a mesh axis runs over, the one named last changes fastest.
Arguments:
- student: bfloat16 [6144, 1024], P(('grp', 'blk')), parts along dimension 0, may hold values from -6 to 6
- teacher: bfloat16 [6144, 1024], P(('grp', 'blk')), parts along dimension 0, may hold values from -6 to 6
Outputs:
- grad_student: float32 [6144, 1024], P(('grp', 'blk')), parts along dimension 0
There are 4 independent parts, one for each index of `grp`. A program takes and returns all parts, laid end to end along the dimension named above; each array names one. Nothing has to cross between parts.
All inputs are finite; a program needn't handle non-finite values.
Results may differ from a plain program's by a relative error of at most 0.01.
Values may be sent and summed in bfloat16 or wider, within the bound.
No kernel may reach another device: no remote copies, remote signals or barrier semaphores. Data moves between devices by JAX's collectives and lax.ppermute only.
A program may use at most 128 MiB of HBM per device.

v0:
```python
import jax
import jax.numpy as jnp
from jax import lax
from jax.sharding import PartitionSpec as P

D = 1024


def normalize(values):
    floats = values.astype(jnp.float32)
    norms = jnp.sqrt(jnp.sum(floats * floats, axis=1, keepdims=True) + 1e-06)
    return (floats / norms, norms)


def split_product(left, right):
    left_hi = left.astype(jnp.bfloat16)
    left_lo = (left - left_hi.astype(jnp.float32)).astype(jnp.bfloat16)
    return jnp.dot(left_hi, right, preferred_element_type=jnp.float32) + jnp.dot(
        left_lo, right, preferred_element_type=jnp.float32
    )


def body(student, teacher):
    row_count = student.shape[0]
    text_count = row_count * lax.axis_size("blk")
    s_float, norm_h = normalize(student)
    s_half = s_float.astype(jnp.bfloat16)
    t_float, teacher_norm = normalize(teacher)
    t_half = t_float.astype(jnp.bfloat16)
    s_wide = s_half.astype(jnp.float32)
    s_piece = lax.all_gather(s_half, "blk", axis=0, tiled=True)
    t_piece = lax.all_gather(t_half, "blk", axis=0, tiled=True)
    gram_s = lax.dot_general(
        s_half, s_piece, (((1,), (1,)), ((), ())), preferred_element_type=jnp.float32
    )
    gram_t = lax.dot_general(
        t_half, t_piece, (((1,), (1,)), ((), ())), preferred_element_type=jnp.float32
    )
    product = split_product(gram_s - gram_t, s_piece)
    g_s = product * (D / jnp.sqrt(jnp.float32(text_count)))
    along = jnp.sum(s_wide * g_s, axis=1, keepdims=True)
    return (g_s - s_wide * along) / norm_h


def solution(mesh):
    in_specs = (P(("grp", "blk"), None), P(("grp", "blk"), None))
    out_specs = P(("grp", "blk"), None)
    return jax.shard_map(body, mesh=mesh, in_specs=in_specs, out_specs=out_specs, check_vma=False)
```

profile of v0, /device:TPU:0, one launch (start us, length us, event | category | flops | bytes accessed | tf_op | source)
XLA Modules:
  0.0 102.9 jit_solution(4346751903632216425)
XLA Ops:
  6.5 0.0 all-gather.3.cloned.1.call-start
  6.5 1.2 %fusion.1 = f32[192]{0:T(256)S(1)} fusion(bf16[192,1024]{1,0:T(8,128)(2,1)} %param.2), kind=kLoop, calls=%fused_computation.10 | loop fusion | flops 589632 | bytes 393984 | tf_op jit(solution)/shard_map/reduce_sum | solution.py:11
  7.7 1.9 %fusion.2 = bf16[192,1024]{1,0:T(8,128)(2,1)} fusion(bf16[192,1024]{1,0:T(8,128)(2,1)} %param.2, f32[192]{0:T(256)S(1)} %add_sqrt_fusion.1), kind=kLoop, calls=%fused_computation.11 | loop fusion | flops 589824 | bytes 787200 | tf_op jit(solution)/shard_map/convert_element_type | solution.py:27
  9.6 0.0 all-gather.3.cloned.1.call-update
  9.6 0.0 all-gather.5.cloned.1.call-start
  9.7 1.2 %fusion.3 = f32[192]{0:T(256)S(1)} fusion(bf16[192,1024]{1,0:T(8,128)(2,1)} %param.3), kind=kLoop, calls=%fused_computation.12 | loop fusion | flops 589632 | bytes 393984 | tf_op jit(solution)/shard_map/reduce_sum | solution.py:11
  10.8 1.9 %fusion.4 = bf16[192,1024]{1,0:T(8,128)(2,1)} fusion(bf16[192,1024]{1,0:T(8,128)(2,1)} %param.3, f32[192]{0:T(256)S(1)} %add_sqrt_fusion), kind=kLoop, calls=%fused_computation.13 | loop fusion | flops 589824 | bytes 787200 | tf_op jit(solution)/shard_map/convert_element_type | solution.py:29
  12.7 0.0 copy-start.2
  12.7 0.0 all-gather.5.cloned.1.call-update
  12.8 38.0 %all-gather.3.cloned.1.call-done = bf16[1536,1024]{1,0:T(8,128)(2,1)} async-done(((bf16[192,1024]{1,0:T(8,128)(2,1)}), bf16[1536,1024]{1,0:T(8,128)(2,1)}) %all-gather.3.cloned.1.call-update) | async-done | bytes 3145744 | tf_op jit(solution)/shard_map/all_gather | solution.py:31
  50.7 4.2 %fusion.11 = f32[192,1536]{1,0:T(8,128)} fusion(bf16[192,1024]{1,0:T(8,128)(2,1)} %fusion.2, bf16[1536,1024]{1,0:T(8,128)(2,1)} %all-gather.3.cloned.1.call-done), kind=kOutput, calls=%fused_computation.22 | convolution fusion | flops 603979776 | bytes 4718592 | tf_op jit(solution)/shard_map/dot_general | solution.py:33
  55.0 0.0 copy-start
  55.0 34.5 %all-gather.5.cloned.1.call-done = bf16[1536,1024]{1,0:T(8,128)(2,1)} async-done(((bf16[192,1024]{1,0:T(8,128)(2,1)}), bf16[1536,1024]{1,0:T(8,128)(2,1)}) %all-gather.5.cloned.1.call-update) | async-done | bytes 3145744 | tf_op jit(solution)/shard_map/all_gather | solution.py:32
  89.5 0.0 copy-done.2
  89.5 3.4 %convolution_subtract_fusion = f32[192,1536]{1,0:T(8,128)S(1)} fusion(f32[192,1536]{1,0:T(8,128)} %fusion.11, bf16[192,1024]{1,0:T(8,128)(2,1)S(1)} %copy-done.2, bf16[1536,1024]{1,0:T(8,128)(2,1)} %all-gather.5.cloned.1.call-done), kind=kOutput, calls=%fused_computation | convolution fusion | flops 604274688 | bytes 5898240 | tf_op jit(solution)/shard_map/dot_general | solution.py:36
  92.9 0.0 copy-done
  92.9 0.0 copy-start.1
  93.0 0.8 fusion.9
  93.8 0.2 copy-done.1
  93.9 0.0 copy-start.3
  93.9 1.0 fusion.5
  94.9 0.0 copy-done.3
  94.9 1.1 %fusion.7 = f32[192,1024]{1,0:T(8,128)} fusion(f32[192,1024]{1,0:T(8,128)S(1)} %get-tuple-element.6, f32[192]{0:T(256)S(1)} %get-tuple-element.5, f32[192]{0:T(256)S(1)} %add_sqrt_fusion.1, bf16[192,1024]{1,0:T(8,128)(2,1)S(1)} %copy-done.3), kind=kLoop, calls=%fused_computation.16 | loop fusion | flops 1376256 | bytes 1967616 | tf_op jit(solution)/shard_map/div | solution.py:42
  (2 shorter events, 0.0 us)
Async XLA Ops:
  6.5 44.2 %all-gather.3.cloned.1.call-start = ((), (), s32[]{:S(2)}) async-start(), calls=%async_computation | async-start | bytes 3538944 | tf_op jit(solution)/shard_map/all_gather | solution.py:31
  9.6 79.9 %all-gather.5.cloned.1.call-start = ((), (), s32[]{:S(2)}) async-start(), calls=%async_computation.1 | async-start | bytes 3538944 | tf_op jit(solution)/shard_map/all_gather | solution.py:32
  12.7 76.8 %copy-start.2 = (bf16[192,1024]{1,0:T(8,128)(2,1)S(1)}, bf16[192,1024]{1,0:T(8,128)(2,1)}, u32[]{:S(2)}) copy-start(bf16[192,1024]{1,0:T(8,128)(2,1)} %fusion.4) | copy-start | bytes 1179652
  55.0 38.0 %copy-start = (bf16[1536,1024]{1,0:T(8,128)(2,1)S(1)}, bf16[1536,1024]{1,0:T(8,128)(2,1)}, u32[]{:S(2)}) copy-start(bf16[1536,1024]{1,0:T(8,128)(2,1)} %all-gather.3.cloned.1.call-done) | copy-start | bytes 9437188
  92.9 1.0 copy-start.1
  93.9 1.0 copy-start.3
Sparse Core Ops, SparseCore 0:
  9.7 40.9 all-gather.2
  52.4 37.1 all-gather.4
where the time goes:
time: 103 us
  waiting for transfers between devices  72.5 us (70%)
  between operations  13.4 us (13%)
  matrix products  9.43 us (9%)
  other arithmetic  7.21 us (7%)
    all_gather x1, waiting for transfers between devices, body(): s_piece = lax.all_gather(s_half, 'blk', axis=0, tiled=True)  38 us
    all_gather x1, waiting for transfers between devices, body(): t_piece = lax.all_gather(t_half, 'blk', axis=0, tiled=True)  34.5 us
    dot_general x1, matrix products, body(): lax.dot_general(s_half, s_piece, (((1,), (1,)), ((), ())), preferred_elem...  4.25 us
    dot_general x1, matrix products, body(): lax.dot_general(t_half, t_piece, (((1,), (1,)), ((), ())), preferred_elem...  3.4 us
    reduce_sum x2, other arithmetic, normalize(): norms = jnp.sqrt(jnp.sum(floats * floats, axis=1, keepdims=True) + 1e-06)  2.31 us
  transfers between devices with their start and end apart: 2, of which 2 were waited for; matrix products, arithmetic and copies ran while one was open for 7% of the time, Pallas kernels for 0%

commit v1 on v0

--- a/solution.py
+++ b/solution.py
@@ -28,7 +28,12 @@
     t_float, teacher_norm = normalize(teacher)
     t_half = t_float.astype(jnp.bfloat16)
     s_wide = s_half.astype(jnp.float32)
-    s_piece = lax.all_gather(s_half, "blk", axis=0, tiled=True)
+    ring = [s_half]
+    for hop in range(7):
+        ring.append(lax.ppermute(ring[-1], "blk", [(dev, (dev + 1) % 8) for dev in range(8)]))
+    s_piece = jnp.roll(
+        jnp.concatenate(ring[::-1], axis=0), (lax.axis_index("blk") + 1) * ring[0].shape[0], axis=0
+    )
     t_piece = lax.all_gather(t_half, "blk", axis=0, tiled=True)
     gram_s = lax.dot_general(
         s_half, s_piece, (((1,), (1,)), ((), ())), preferred_element_type=jnp.float32

time: 103 us -> 129 us (1.25)
  local copies, waits for them, and re-layouts: 0.2 us -> 13 us
  waiting for transfers between devices: 72.5 us -> 80.7 us
  matrix products: 9.43 us -> 12.2 us
    ppermute x0 -> x7, waiting for transfers between devices: none -> 80.7 us  [body(): lax.ppermute(ring[-1], 'blk', [(dev, (dev + 1) % 8) for dev in range(8)])]
    all_gather x1 -> x0, waiting for transfers between devices: 38 us -> none  [body(): s_piece = lax.all_gather(s_half, 'blk', axis=0, tiled=True)]
    all_gather x1, waiting for transfers between devices: 34.5 us -> 0.01 us  [body(): t_piece = lax.all_gather(t_half, 'blk', axis=0, tiled=True)]
    unnamed x8 -> x18, local copies, waits for them, and re-layouts: 0.2 us -> 13 us
    dot_general x1, matrix products: 0.8 us -> 3.1 us  [split_product(): jnp.dot(left_hi, right, preferred_element_type=jnp.float32)]
    dot_general x1, matrix products: 0.98 us -> 2.92 us  [split_product(): jnp.dot(left_lo, right, preferred_element_type=jnp.float32)]
  transfers between devices with their start and end apart: 2 -> 8, of which waited for: 2 -> 7; matrix products, arithmetic and copies ran while one was open for 7% -> 13% of each run, Pallas kernels for 0% -> 0%
where the time goes in v1:
time: 129 us; the launch traced here: 128 us
  waiting for transfers between devices  80.7 us (63%)
  between operations  13.4 us (10%)
  local copies, waits for them, and re-layouts  13 us (10%)
  matrix products  12.2 us (9%)
  other arithmetic  8.35 us (6%)
    ppermute x7, waiting for transfers between devices, body(): lax.ppermute(ring[-1], 'blk', [(dev, (dev + 1) % 8) for dev in range(8)])  80.7 us
    unnamed x18, local copies, waits for them, and re-layouts  13 us
    dot_general x1, matrix products, body(): lax.dot_general(s_half, s_piece, (((1,), (1,)), ((), ())), preferred_elem...  3.11 us
    dot_general x1, matrix products, split_product(): jnp.dot(left_hi, right, preferred_element_type=jnp.float32)  3.1 us
    dot_general x1, matrix products, body(): lax.dot_general(t_half, t_piece, (((1,), (1,)), ((), ())), preferred_elem...  3.07 us
    dot_general x1, matrix products, split_product(): jnp.dot(left_lo, right, preferred_element_type=jnp.float32)  2.92 us
  transfers between devices with their start and end apart: 8, of which 7 were waited for; matrix products, arithmetic and copies ran while one was open for 13% of the time, Pallas kernels for 0%

profile of v1, /device:TPU:0, one launch (start us, length us, event | category | flops | bytes accessed | tf_op | source)
XLA Modules:
  0.0 128.2 jit_solution(355845835469750470)
XLA Ops:
  6.5 1.2 fusion.13
  7.8 1.9 %fusion.14 = bf16[192,1024]{1,0:T(8,128)(2,1)} fusion(bf16[192,1024]{1,0:T(8,128)(2,1)} %param.3, f32[192]{0:T(256)S(1)} %add_sqrt_fusion), kind=kLoop, calls=%fused_computation.18 | loop fusion | flops 589824 | bytes 787200 | tf_op jit(solution)/shard_map/convert_element_type | solution.py:29
  9.7 1.2 fusion.11
  10.8 1.2 fusion.12
  12.5 9.5 %collective-permute-done = bf16[192,1024]{1,0:T(8,128)(2,1)S(1)} collective-permute-done((bf16[192,1024]{1,0:T(8,128)(2,1)S(1)}, bf16[192,1024]{1,0:T(8,128)(2,1)S(1)}, u32[]{:S(2)}, u32[]{:S(2)}) %collective-permute-start) | collective-permute-done | bytes 393248 | tf_op jit(solution)/shard_map/ppermute | solution.py:33
  22.0 17.6 %collective-permute-done.1 = bf16[192,1024]{1,0:T(8,128)(2,1)S(1)} collective-permute-done((bf16[192,1024]{1,0:T(8,128)(2,1)S(1)}, bf16[192,1024]{1,0:T(8,128)(2,1)S(1)}, u32[]{:S(2)}, u32[]{:S(2)}) %collective-permute-start.1) | collective-permute-done | bytes 393248 | tf_op jit(solution)/shard_map/ppermute | solution.py:33
  39.6 17.5 %collective-permute-done.2 = bf16[192,1024]{1,0:T(8,128)(2,1)S(1)} collective-permute-done((bf16[192,1024]{1,0:T(8,128)(2,1)S(1)}, bf16[192,1024]{1,0:T(8,128)(2,1)S(1)}, u32[]{:S(2)}, u32[]{:S(2)}) %collective-permute-start.2) | collective-permute-done | bytes 393248 | tf_op jit(solution)/shard_map/ppermute | solution.py:33
  57.1 9.0 %collective-permute-done.3 = bf16[192,1024]{1,0:T(8,128)(2,1)S(1)} collective-permute-done((bf16[192,1024]{1,0:T(8,128)(2,1)S(1)}, bf16[192,1024]{1,0:T(8,128)(2,1)S(1)}, u32[]{:S(2)}, u32[]{:S(2)}) %collective-permute-start.3) | collective-permute-done | bytes 393248 | tf_op jit(solution)/shard_map/ppermute | solution.py:33
  66.1 9.0 %collective-permute-done.4 = bf16[192,1024]{1,0:T(8,128)(2,1)S(1)} collective-permute-done((bf16[192,1024]{1,0:T(8,128)(2,1)S(1)}, bf16[192,1024]{1,0:T(8,128)(2,1)S(1)}, u32[]{:S(2)}, u32[]{:S(2)}) %collective-permute-start.4) | collective-permute-done | bytes 393248 | tf_op jit(solution)/shard_map/ppermute | solution.py:33
  75.1 9.0 %collective-permute-done.5 = bf16[192,1024]{1,0:T(8,128)(2,1)S(1)} collective-permute-done((bf16[192,1024]{1,0:T(8,128)(2,1)S(1)}, bf16[192,1024]{1,0:T(8,128)(2,1)S(1)}, u32[]{:S(2)}, u32[]{:S(2)}) %collective-permute-start.5) | collective-permute-done | bytes 393248 | tf_op jit(solution)/shard_map/ppermute | solution.py:33
  84.1 9.1 %collective-permute-done.6 = bf16[192,1024]{1,0:T(8,128)(2,1)} collective-permute-done((bf16[192,1024]{1,0:T(8,128)(2,1)S(1)}, bf16[192,1024]{1,0:T(8,128)(2,1)}, u32[]{:S(2)}, u32[]{:S(2)}) %collective-permute-start.6) | collective-permute-done | bytes 393248 | tf_op jit(solution)/shard_map/ppermute | solution.py:33
  93.2 1.8 %constant_dynamic-update-slice_fusion.15 = bf16[3072,1024]{1,0:T(8,128)(2,1)} fusion(bf16[192,1024]{1,0:T(8,128)(2,1)} %collective-permute-done.6), kind=kLoop, calls=%fused_computation.39 | loop fusion | bytes 786432
  95.0 0.8 constant_dynamic-update-slice_fusion.14
  95.8 0.8 constant_dynamic-update-slice_fusion.13
  96.6 0.8 constant_dynamic-update-slice_fusion.12
  97.4 0.8 constant_dynamic-update-slice_fusion.11
  98.1 0.8 constant_dynamic-update-slice_fusion.10
  99.0 0.8 constant_dynamic-update-slice_fusion.9
  99.7 0.9 constant_dynamic-update-slice_fusion.8
  100.7 1.8 %constant_dynamic-update-slice_fusion.7 = bf16[3072,1024]{1,0:T(8,128)(2,1)} fusion(bf16[3072,1024]{1,0:T(8,128)(2,1)} %constant_dynamic-update-slice_fusion.8, bf16[192,1024]{1,0:T(8,128)(2,1)} %collective-permute-done.6), kind=kLoop, calls=%fused_computation.31 | loop fusion | bytes 786432
  102.4 0.8 constant_dynamic-update-slice_fusion.6
  103.2 0.8 constant_dynamic-update-slice_fusion.5
  104.0 0.8 constant_dynamic-update-slice_fusion.4
  104.8 0.8 constant_dynamic-update-slice_fusion.3
  105.6 0.8 constant_dynamic-update-slice_fusion.2
  106.3 0.8 constant_dynamic-update-slice_fusion.1
  107.2 0.9 constant_dynamic-update-slice_fusion
  108.1 3.1 %fusion.23 = f32[192,1536]{1,0:T(8,128)S(1)} fusion(bf16[192,1024]{1,0:T(8,128)(2,1)S(1)} %copy-done.1, bf16[1536,1024]{1,0:T(8,128)(2,1)} %all-gather.2.cloned.1.call-done), kind=kOutput, calls=%fused_computation.45 | convolution fusion | flops 603979776 | bytes 4718592 | tf_op jit(solution)/shard_map/dot_general | solution.py:41
  111.1 3.1 %convolution_subtract_fusion = f32[192,1536]{1,0:T(8,128)S(1)} fusion(f32[192,1536]{1,0:T(8,128)S(1)} %fusion.23, bf16[192,1024]{1,0:T(8,128)(2,1)S(1)} %fusion.12, bf16[3072,1024]{1,0:T(8,128)(2,1)} %constant_dynamic-update-slice_fusion, s32[]{:T(128)S(6)} %select_n.14), kind=kOutput, calls=%fused_computation | convolution fusion | flops 604274688 | bytes 5898244 | tf_op jit(solution)/shard_map/dot_general | solution.py:38
  114.2 2.9 %fusion = f32[192,1024]{1,0:T(8,128)S(1)} fusion(bf16[3072,1024]{1,0:T(8,128)(2,1)} %constant_dynamic-update-slice_fusion, s32[]{:T(128)S(6)} %select_n.14, f32[192,1536]{1,0:T(8,128)S(1)} %convolution_subtract_fusion), kind=kOutput, calls=%fused_computation.1 | convolution fusion | flops 605159424 | bytes 5111812 | tf_op jit(solution)/shard_map/dot_general | solution.py:18
  117.2 3.1 %fusion.15 = (f32[192]{0:T(256)S(1)}, f32[192,1024]{1,0:T(8,128)S(1)}) fusion(bf16[192,1024]{1,0:T(8,128)(2,1)S(1)} %fusion.12, f32[192,1024]{1,0:T(8,128)S(1)} %fusion, bf16[3072,1024]{1,0:T(8,128)(2,1)} %constant_dynamic-update-slice_fusion, s32[]{:T(128)S(6)} %select_n.14, f32[192,1536]{1,0:T(8,128)S(1)} %convolution_subtract_fusion), kind=kOutput, calls=%fused_computation.19 | convolution fusion | flops 605257536 | bytes 6292228 | tf_op jit(solution)/shard_map/dot_general | solution.py:18
  120.3 1.1 fusion.17
  (16 shorter events, 0.6 us)
Async XLA Ops:
  6.5 93.2 %copy-start = (bf16[192,1024]{1,0:T(8,128)(2,1)S(1)}, bf16[192,1024]{1,0:T(8,128)(2,1)}, u32[]{:S(2)}) copy-start(bf16[192,1024]{1,0:T(8,128)(2,1)} %param.2) | copy-start | bytes 1179652
  6.5 101.5 %all-gather.2.cloned.1.call-start = ((), (), s32[]{:S(2)}) async-start(), calls=%async_computation | async-start | bytes 3538944 | tf_op jit(solution)/shard_map/all_gather | solution.py:37
  12.0 10.0 %collective-permute-start = (bf16[192,1024]{1,0:T(8,128)(2,1)S(1)}, bf16[192,1024]{1,0:T(8,128)(2,1)S(1)}, u32[]{:S(2)}, u32[]{:S(2)}) collective-permute-start(bf16[192,1024]{1,0:T(8,128)(2,1)S(1)} %fusion.12), channel_id=1, source_target_pairs={{0,1},{1,2},{2,3},{3,4},{4,5},{5,6},{6,7},{7,0},{8,9},{9,10},{10,1... | collective-permute-start | bytes 1179656 | tf_op jit(solution)/shard_map/ppermute | solution.py:33
  22.0 17.6 %collective-permute-start.1 = (bf16[192,1024]{1,0:T(8,128)(2,1)S(1)}, bf16[192,1024]{1,0:T(8,128)(2,1)S(1)}, u32[]{:S(2)}, u32[]{:S(2)}) collective-permute-start(bf16[192,1024]{1,0:T(8,128)(2,1)S(1)} %collective-permute-done), channel_id=1, source_target_pairs={{0,1},{1,2},{2,3},{3,4},{4,5},{5,6},{6,7},{7,0},{8,9},{9,10},{10,1... | collective-permute-start | bytes 1179656 | tf_op jit(solution)/shard_map/ppermute | solution.py:33
  39.6 17.6 %collective-permute-start.2 = (bf16[192,1024]{1,0:T(8,128)(2,1)S(1)}, bf16[192,1024]{1,0:T(8,128)(2,1)S(1)}, u32[]{:S(2)}, u32[]{:S(2)}) collective-permute-start(bf16[192,1024]{1,0:T(8,128)(2,1)S(1)} %collective-permute-done.1), channel_id=1, source_target_pairs={{0,1},{1,2},{2,3},{3,4},{4,5},{5,6},{6,7},{7,0},{8,9},{9,10},{10,1... | collective-permute-start | bytes 1179656 | tf_op jit(solution)/shard_map/ppermute | solution.py:33
  57.1 9.0 %collective-permute-start.3 = (bf16[192,1024]{1,0:T(8,128)(2,1)S(1)}, bf16[192,1024]{1,0:T(8,128)(2,1)S(1)}, u32[]{:S(2)}, u32[]{:S(2)}) collective-permute-start(bf16[192,1024]{1,0:T(8,128)(2,1)S(1)} %collective-permute-done.2), channel_id=1, source_target_pairs={{0,1},{1,2},{2,3},{3,4},{4,5},{5,6},{6,7},{7,0},{8,9},{9,10},{10,1... | collective-permute-start | bytes 1179656 | tf_op jit(solution)/shard_map/ppermute | solution.py:33
  66.1 9.0 %collective-permute-start.4 = (bf16[192,1024]{1,0:T(8,128)(2,1)S(1)}, bf16[192,1024]{1,0:T(8,128)(2,1)S(1)}, u32[]{:S(2)}, u32[]{:S(2)}) collective-permute-start(bf16[192,1024]{1,0:T(8,128)(2,1)S(1)} %collective-permute-done.3), channel_id=1, source_target_pairs={{0,1},{1,2},{2,3},{3,4},{4,5},{5,6},{6,7},{7,0},{8,9},{9,10},{10,1... | collective-permute-start | bytes 1179656 | tf_op jit(solution)/shard_map/ppermute | solution.py:33
  75.1 9.0 %collective-permute-start.5 = (bf16[192,1024]{1,0:T(8,128)(2,1)S(1)}, bf16[192,1024]{1,0:T(8,128)(2,1)S(1)}, u32[]{:S(2)}, u32[]{:S(2)}) collective-permute-start(bf16[192,1024]{1,0:T(8,128)(2,1)S(1)} %collective-permute-done.4), channel_id=1, source_target_pairs={{0,1},{1,2},{2,3},{3,4},{4,5},{5,6},{6,7},{7,0},{8,9},{9,10},{10,1... | collective-permute-start | bytes 1179656 | tf_op jit(solution)/shard_map/ppermute | solution.py:33
  84.1 9.1 %collective-permute-start.6 = (bf16[192,1024]{1,0:T(8,128)(2,1)S(1)}, bf16[192,1024]{1,0:T(8,128)(2,1)}, u32[]{:S(2)}, u32[]{:S(2)}) collective-permute-start(bf16[192,1024]{1,0:T(8,128)(2,1)S(1)} %collective-permute-done.5), channel_id=1, source_target_pairs={{0,1},{1,2},{2,3},{3,4},{4,5},{5,6},{6,7},{7,0},{8,9},{9,10},{10,1... | collective-permute-start | bytes 1179656 | tf_op jit(solution)/shard_map/ppermute | solution.py:33
  84.1 23.9 %copy-start.1 = (bf16[192,1024]{1,0:T(8,128)(2,1)S(1)}, bf16[192,1024]{1,0:T(8,128)(2,1)}, u32[]{:S(2)}) copy-start(bf16[192,1024]{1,0:T(8,128)(2,1)} %fusion.14) | copy-start | bytes 1179652
Sparse Core Ops, SparseCore 0:
  9.8 49.3 all-gather.1
